TPU v7x, 512 devices: a whole 4x8x8 slice. The times are simulated.
512 devices in a mesh: frames: 32 (over x, y_lo, core), book: 16 (over z, y_hi).
Axes of the slice: x: 4, y: 8 (y_hi: 2, y_lo: 4; y = y_hi * 4 + y_lo), z: 8, core: 2. Of those that a mesh axis runs over, the one named last changes fastest.
Arguments:
- gate_pre: bfloat16 [8192, 6144], P('frames', 'book'), may hold values from -6 to 6
- up_pre: bfloat16 [8192, 6144], P('frames', 'book'), may hold values from -6 to 6
- down_weight: bfloat16 [6144, 4096], P('book'), may hold values from -0.109375 to 0.109375
- residual: bfloat16 [8192, 4096], P('frames', 'book'), may hold values from -6 to 6
- out_gain: bfloat16 [4096], replicated, may hold values from 0.25 to 1.75
- in_proj: bfloat16 [16, 4096, 1024], P('book', 'frames'), may hold values from -0.09375 to 0.09375
- embedding: bfloat16 [16, 1024, 1024], P('book', 'frames'), may hold values from -6 to 6
- token_ids: int32 [8192, 16], P('frames', 'book'), may hold values from 0 to 1023
- depth_gain: bfloat16 [16, 1024], P('book'), may hold values from 0.25 to 1.75
- qkv_weight: bfloat16 [16, 1024, 1536], P('book', 'frames'), may hold values from -2 to 2
Outputs:
- context: bfloat16 [8192, 16, 512], P(('frames', 'book'))
All inputs are finite; a program needn't handle non-finite values.
Results may differ from a plain program's by a relative error of at most 0.019.
Values may be sent and summed in bfloat16 or wider, within the bound.
A program may use at most 64 MiB of HBM per device.

v0:
```python
import jax
import jax.numpy as jnp
from jax import lax
from jax.sharding import Mesh
from jax.sharding import PartitionSpec as P

H = 8
HD = 64
BOOK = ("book_0", "book_1")
FRAMES_BOOK = ("frames", "book_0", "book_1")


def sum_by_axis(shard, axes, dim):
    if not axes:
        return shard
    nearer = lax.psum_scatter(shard, axes[0], scatter_dimension=dim, tiled=True)
    return sum_by_axis(nearer, axes[1:], dim)


def rms_scale(values, gain):
    moment = jnp.mean(values * values, axis=-1, keepdims=True)
    return values * lax.rsqrt(moment + 1e-05) * gain


def attend_block(grouped):
    inner = grouped[0]
    frames_here = inner.shape[0]
    books = inner.shape[1]
    width = H * HD
    queries = inner[:, :, :width].reshape(frames_here, books, H, HD)
    keys_all = inner[:, :, width : 2 * width].reshape(frames_here, books, H, HD)
    values_all = inner[:, :, 2 * width :].reshape(frames_here, books, H, HD)
    scores = jnp.einsum(
        "nkhd,njhd->nhkj", queries, keys_all, preferred_element_type=jnp.float32
    ) * HD ** (-0.5)
    causal = lax.broadcasted_iota(jnp.int32, (books, books), 0) >= lax.broadcasted_iota(
        jnp.int32, (books, books), 1
    )
    scores = jnp.where(causal, scores, -1e30)
    peak = jnp.max(scores, axis=-1, keepdims=True)
    expo = jnp.exp(scores - peak)
    probability = (expo / jnp.sum(expo, axis=-1, keepdims=True)).astype(jnp.bfloat16)
    context = jnp.einsum(
        "nhkj,njhd->nkhd", probability, values_all, preferred_element_type=jnp.float32
    )
    return context.reshape(1, frames_here, books, width).astype(jnp.bfloat16)


def gather_embedding(embedding, token_column):
    table_piece = lax.all_gather(embedding, "frames", axis=1, tiled=True)
    columns = lax.broadcasted_iota(jnp.int32, (1, table_piece.shape[1]), 1)
    matches = (token_column[:, None] == columns).astype(jnp.bfloat16)
    return jnp.dot(matches, table_piece[0], preferred_element_type=jnp.float32)


def per_device(
    gate_pre,
    up_pre,
    down_weight,
    residual,
    out_gain,
    in_proj,
    embedding,
    token_ids,
    depth_gain,
    qkv_weight,
):
    tokens_here = gate_pre.shape[0]
    book_count = lax.axis_size(BOOK)
    token_column = token_ids[:, 0]
    hidden = (jax.nn.silu(gate_pre.astype(jnp.float32)) * up_pre.astype(jnp.float32)).astype(
        jnp.bfloat16
    )
    partial_value = jnp.dot(hidden, down_weight, preferred_element_type=jnp.float32)
    share = sum_by_axis(partial_value, BOOK, 1)
    temporal = (share + residual.astype(jnp.float32)).astype(jnp.bfloat16)
    whole = lax.all_gather(temporal, BOOK, axis=1, tiled=True)
    normed = rms_scale(whole.astype(jnp.float32), out_gain.astype(jnp.float32)).astype(jnp.bfloat16)
    looked = gather_embedding(embedding, token_column)
    columns = normed
    projected = jnp.dot(
        columns,
        lax.all_gather(in_proj, "frames", axis=1, tiled=True)[0],
        preferred_element_type=jnp.float32,
    )
    depth_in = (projected + looked).astype(jnp.bfloat16)
    depth_normed = rms_scale(
        depth_in.astype(jnp.float32), depth_gain[0].astype(jnp.float32)
    ).astype(jnp.bfloat16)
    columns = depth_normed
    packed = jnp.dot(
        columns,
        lax.all_gather(qkv_weight, "frames", axis=1, tiled=True)[0],
        preferred_element_type=jnp.float32,
    ).astype(jnp.bfloat16)
    grouped = packed.reshape(book_count, tokens_here // book_count, 1, packed.shape[1])
    context = attend_block(lax.all_to_all(grouped, BOOK, split_axis=0, concat_axis=2, tiled=True))
    return context.reshape(context.shape[1], context.shape[2], context.shape[3])


def solution(mesh):
    split = Mesh(mesh.devices.reshape(mesh.shape["frames"], 8, 2), ("frames", "book_0", "book_1"))
    placed = (
        P("frames", BOOK),
        P("frames", BOOK),
        P(BOOK, None),
        P("frames", BOOK),
        P(),
        P(BOOK, "frames", None),
        P(BOOK, "frames", None),
        P("frames", BOOK),
        P(BOOK, None),
        P(BOOK, "frames", None),
    )
    return jax.shard_map(
        per_device,
        mesh=split,
        in_specs=placed,
        out_specs=P(FRAMES_BOOK, None, None),
        check_vma=False,
    )
```

profile of v0, /device:TPU:40, one launch (start us, length us, event | category | flops | bytes accessed | tf_op | source)
XLA Modules:
  0.0 474.8 jit_solution(13796978290205377564)
XLA Ops:
  6.5 0.0 copy-start
  6.5 0.0 reduce-scatter.3.cloned.1.call-start
  6.5 1.9 copy-done
  8.4 4.3 fusion.42
  12.7 0.0 copy-start.1
  12.7 0.0 copy-start.2
  12.7 0.0 copy-start.3
  12.7 0.0 reduce-scatter.3.cloned.1.call-update
  12.7 0.0 reduce-scatter.5.cloned.1.call-start
  12.8 63.1 %reduce-scatter.3.cloned.1.call-done = f32[256,512]{1,0:T(8,128)} async-done(((f32[256,4096]{1,0:T(8,128)}), f32[256,512]{1,0:T(8,128)}) %reduce-scatter.3.cloned.1.call-update) | async-done | bytes 524304 | tf_op jit(solution)/shard_map/reduce_scatter | solution.py:16
  75.8 0.0 reduce-scatter.5.cloned.1.call-update
  75.8 0.0 all-gather.5.cloned.1.call-start
  75.9 28.9 %reduce-scatter.5.cloned.1.call-done = f32[256,256]{1,0:T(8,128)} async-done(((f32[256,512]{1,0:T(8,128)}), f32[256,256]{1,0:T(8,128)}) %reduce-scatter.5.cloned.1.call-update) | async-done | bytes 262160 | tf_op jit(solution)/shard_map/reduce_scatter | solution.py:16
  104.8 0.0 copy-done.1
  104.8 1.6 add_convert_fusion
  106.4 0.0 all-gather.5.cloned.1.call-update
  106.4 0.0 all-gather.7.cloned.1.call-start
  106.5 0.5 all-gather.7.cloned.1.call-update
  107.0 0.0 all-gather.9.cloned.1.call-start
  107.0 0.5 all-gather.9.cloned.1.call-update
  107.6 0.0 all-gather.11.cloned.1.call-start
  107.6 0.5 all-gather.11.cloned.1.call-update
  108.2 0.0 copy-done.2
  108.2 0.0 copy-done.3
  108.2 101.6 %all-gather.5.cloned.1.call-done = bf16[256,4096]{1,0:T(8,128)(2,1)} async-done(((bf16[256,256]{1,0:T(8,128)(2,1)}), bf16[256,4096]{1,0:T(8,128)(2,1)}) %all-gather.5.cloned.1.call-update) | async-done | bytes 2097168 | tf_op jit(solution)/shard_map/all_gather | solution.py:77
  209.8 2.1 fusion.3
  211.9 0.0 copy-start.4
  211.9 68.1 %all-gather.7.cloned.1.call-done = bf16[1,4096,1024]{2,1,0:T(8,128)(2,1)} async-done(((bf16[1,128,1024]{2,1,0:T(8,128)(2,1)}), bf16[1,4096,1024]{2,1,0:T(8,128)(2,1)}) %all-gather.7.cloned.1.call-update) | async-done | bytes 8388624 | tf_op jit(solution)/shard_map/all_gather | solution.py:83
  280.0 7.4 %fusion.1 = f32[256,1024]{1,0:T(8,128)} fusion(bf16[1,4096,1024]{2,1,0:T(8,128)(2,1)} %all-gather.7.cloned.1.call-done, bf16[256,4096]{1,0:T(8,128)(2,1)} %all-gather.5.cloned.1.call-done, f32[4096]{0:T(1024)S(1)} %convert_element_type.60, f32[256]{0:T(256)S(1)} %add_rsqrt_fusion.1), kind=kOutput, calls=%fused_computation.1 | convolution fusion | flops 2151677952 | bytes 11551744 | tf_op jit(solution)/shard_map/dot_general | solution.py:81
  287.4 55.8 %all-gather.9.cloned.1.call-done = bf16[1,1024,1024]{2,1,0:T(8,128)(2,1)} async-done(((bf16[1,32,1024]{2,1,0:T(8,128)(2,1)}), bf16[1,1024,1024]{2,1,0:T(8,128)(2,1)}) %all-gather.9.cloned.1.call-update) | async-done | bytes 2097168 | tf_op jit(solution)/shard_map/all_gather | solution.py:50
  343.2 0.0 copy-done.4
  343.2 3.4 fusion.26
  346.6 61.3 %all-gather.11.cloned.1.call-done = bf16[1,1024,1536]{2,1,0:T(8,128)(2,1)} async-done(((bf16[1,32,1536]{2,1,0:T(8,128)(2,1)}), bf16[1,1024,1536]{2,1,0:T(8,128)(2,1)}) %all-gather.11.cloned.1.call-update) | async-done | bytes 3145744 | tf_op jit(solution)/shard_map/all_gather | solution.py:93
  407.9 4.0 fusion.8
  411.9 12.8 %all-to-all-start = ((bf16[16,16,1,1536]{3,1,2,0:T(8,128)(2,1)}), bf16[16,16,1,1536]{3,1,2,0:T(8,128)(2,1)}, u32[]{:S(2)}, u32[]{:S(2)}) async-start(bf16[16,16,1,1536]{3,1,2,0:T(8,128)(2,1)} %bitcast.38), calls=%async_computation.2 | async-start | bytes 1572864 | tf_op jit(solution)/shard_map/all_to_all | solution.py:97
  424.7 28.0 %all-to-all-done = bf16[16,16,1,1536]{3,1,2,0:T(8,128)(2,1)} async-done(((bf16[16,16,1,1536]{3,1,2,0:T(8,128)(2,1)}), bf16[16,16,1,1536]{3,1,2,0:T(8,128)(2,1)}, u32[]{:S(2)}, u32[]{:S(2)}) %all-to-all-start) | async-done | bytes 786464 | tf_op jit(solution)/shard_map/all_to_all | solution.py:97
  452.6 2.0 fusion.46
  454.6 2.1 reshape.45
  456.7 2.1 reshape.46
  458.8 1.1 reshape.44
  459.9 3.2 fusion.47
  463.0 1.9 fusion.25
  464.9 0.9 copy.26
  465.9 2.1 convert_element_type.69
  (5 shorter events, 0.0 us)
Async XLA Ops:
  6.5 1.9 copy-start
  6.5 69.3 %reduce-scatter.3.cloned.1.call-start = ((), (), s32[]{:S(2)}) async-start(), calls=%async_computation.3 | async-start | bytes 4718592 | tf_op jit(solution)/shard_map/reduce_scatter | solution.py:16
  12.7 92.1 %copy-start.1 = (bf16[256,256]{1,0:T(8,128)(2,1)S(1)}, bf16[256,256]{1,0:T(8,128)(2,1)}, u32[]{:S(2)}) copy-start(bf16[256,256]{1,0:T(8,128)(2,1)} %param.13) | copy-start | bytes 393220
  12.7 95.5 %copy-start.2 = (bf16[4096]{0:T(1024)(128)(2,1)S(1)}, bf16[4096]{0:T(1024)(128)(2,1)}, u32[]{:S(2)}) copy-start(bf16[4096]{0:T(1024)(128)(2,1)} %param.14) | copy-start | bytes 24580
  12.7 95.5 %copy-start.3 = (bf16[1,1024]{1,0:T(2,128)(2,1)S(1)}, bf16[1,1024]{1,0:T(2,128)(2,1)}, u32[]{:S(2)}) copy-start(bf16[1,1024]{1,0:T(2,128)(2,1)} %param.18) | copy-start | bytes 6148
  12.7 92.1 %reduce-scatter.5.cloned.1.call-start = ((), (), s32[]{:S(2)}) async-start(), calls=%async_computation.4 | async-start | bytes 786432 | tf_op jit(solution)/shard_map/reduce_scatter | solution.py:16
  75.8 133.9 %all-gather.5.cloned.1.call-start = ((), (), s32[]{:S(2)}) async-start(), calls=%async_computation.5 | async-start | bytes 2228224 | tf_op jit(solution)/shard_map/all_gather | solution.py:77
  106.4 173.6 %all-gather.7.cloned.1.call-start = ((), (), s32[]{:S(2)}) async-start(), calls=%async_computation.6 | async-start | bytes 8650752 | tf_op jit(solution)/shard_map/all_gather | solution.py:83
  107.0 236.2 %all-gather.9.cloned.1.call-start = ((), (), s32[]{:S(2)}) async-start(), calls=%async_computation.7 | async-start | bytes 2162688 | tf_op jit(solution)/shard_map/all_gather | solution.py:50
  107.6 300.3 %all-gather.11.cloned.1.call-start = ((), (), s32[]{:S(2)}) async-start(), calls=%async_computation.8 | async-start | bytes 3244032 | tf_op jit(solution)/shard_map/all_gather | solution.py:93
  211.9 131.3 %copy-start.4 = (s32[256,1]{0,1:T(1,128)S(1)}, s32[256,1]{0,1:T(1,128)}, u32[]{:S(2)}) copy-start(s32[256,1]{0,1:T(1,128)} %param.17) | copy-start | bytes 3076
  411.9 40.7 %all-to-all-start = ((bf16[16,16,1,1536]{3,1,2,0:T(8,128)(2,1)}), bf16[16,16,1,1536]{3,1,2,0:T(8,128)(2,1)}, u32[]{:S(2)}, u32[]{:S(2)}) async-start(bf16[16,16,1,1536]{3,1,2,0:T(8,128)(2,1)} %bitcast.38), calls=%async_computation.2 | async-start | bytes 1572864 | tf_op jit(solution)/shard_map/all_to_all | solution.py:97
Sparse Core Ops, SparseCore 0:
  12.8 62.9 reduce-scatter.2
  78.6 26.1 reduce-scatter.4
  107.8 101.8 all-gather.4
  211.8 68.1 all-gather.6
  282.0 61.1 all-gather.8
  345.2 62.6 all-gather.10
where the time goes:
time: 475 us
  waiting for transfers between devices  408 us (86%)
  matrix products  24.1 us (5%)
  between operations  13.5 us (3%)
  starting transfers between devices  13 us (3%)
  local copies, waits for them, and re-layouts  12.1 us (3%)
    all_gather x1, waiting for transfers between devices, per_device(): whole = lax.all_gather(temporal, BOOK, axis=1, tiled=True)  102 us
    reduce_scatter x2, waiting for transfers between devices, sum_by_axis(): nearer = lax.psum_scatter(shard, axes[0], scatter_dimension=dim, tiled=True)  91.9 us
    all_gather x1, waiting for transfers between devices, per_device(): lax.all_gather(in_proj, 'frames', axis=1, tiled=True)[0]  68.1 us
    all_gather x1, waiting for transfers between devices, per_device(): lax.all_gather(qkv_weight, 'frames', axis=1, tiled=True)[0]  61.3 us
    all_gather x1, waiting for transfers between devices, gather_embedding(): table_piece = lax.all_gather(embedding, 'frames', axis=1, tiled=True)  55.8 us
    all_to_all x1, waiting for transfers between devices, per_device(): lax.all_to_all(grouped, BOOK, split_axis=0, concat_axis=2, tiled=True)  28 us
    all_to_all x1, starting transfers between devices, per_device(): lax.all_to_all(grouped, BOOK, split_axis=0, concat_axis=2, tiled=True)  12.8 us
  transfers between devices with their start and end apart: 7, of which 7 were waited for; matrix products, arithmetic and copies ran while one was open for 3% of the time, Pallas kernels for 0%

commit v1 on v0

--- a/solution.py
+++ b/solution.py
@@ -3,11 +3,19 @@
 from jax import lax
 from jax.sharding import Mesh
 from jax.sharding import PartitionSpec as P
+from jax.lax import all_to_all, axis_size
 
 H = 8
 HD = 64
 BOOK = ("book_0", "book_1")
 FRAMES_BOOK = ("frames", "book_0", "book_1")
+
+
+def refer_racks_in(m, comm_axis):
+    return jnp.concatenate(
+        all_to_all(jnp.stack([m] * axis_size(comm_axis)), comm_axis, split_axis=0, concat_axis=0),
+        axis=1,
+    )
 
 
 def sum_by_axis(shard, axes, dim):
@@ -74,7 +82,7 @@
     partial_value = jnp.dot(hidden, down_weight, preferred_element_type=jnp.float32)
     share = sum_by_axis(partial_value, BOOK, 1)
     temporal = (share + residual.astype(jnp.float32)).astype(jnp.bfloat16)
-    whole = lax.all_gather(temporal, BOOK, axis=1, tiled=True)
+    whole = refer_racks_in(temporal, BOOK)
     normed = rms_scale(whole.astype(jnp.float32), out_gain.astype(jnp.float32)).astype(jnp.bfloat16)
     looked = gather_embedding(embedding, token_column)
     columns = normed

time: 475 us -> 409 us (0.86)
  waiting for transfers between devices: 408 us -> 324 us
  starting transfers between devices: 13 us -> 25.7 us
    all_gather x1 -> x0, waiting for transfers between devices: 102 us -> none  [per_device(): whole = lax.all_gather(temporal, BOOK, axis=1, tiled=True)]
    all_to_all x0 -> x1, waiting for transfers between devices: none -> 68.8 us  [refer_racks_in(): all_to_all(jnp.stack([m] * axis_size(comm_axis)), comm_axis, split_axis=0...]
    all_gather x1, waiting for transfers between devices: 68.1 us -> 4.79 us  [per_device(): lax.all_gather(in_proj, 'frames', axis=1, tiled=True)[0]]
    all_gather x1, waiting for transfers between devices: 55.8 us -> 69 us  [gather_embedding(): table_piece = lax.all_gather(embedding, 'frames', axis=1, tiled=True)]
    all_to_all x0 -> x1, starting transfers between devices: none -> 12.7 us  [refer_racks_in(): all_to_all(jnp.stack([m] * axis_size(comm_axis)), comm_axis, split_axis=0...]
  transfers between devices with their start and end apart: 7 -> 7, of which waited for: 7 -> 7; matrix products, arithmetic and copies ran while one was open for 3% -> 5% of each run, Pallas kernels for 0% -> 0%
where the time goes in v1:
time: 409 us
  waiting for transfers between devices  324 us (79%)
  starting transfers between devices  25.7 us (6%)
  matrix products  24.1 us (6%)
  between operations  15.1 us (4%)
  local copies, waits for them, and re-layouts  13.7 us (3%)
  other arithmetic  6.13 us (1%)
    reduce_scatter x2, waiting for transfers between devices, sum_by_axis(): nearer = lax.psum_scatter(shard, axes[0], scatter_dimension=dim, tiled=True)  90.5 us
    all_gather x1, waiting for transfers between devices, gather_embedding(): table_piece = lax.all_gather(embedding, 'frames', axis=1, tiled=True)  69 us
    all_to_all x1, waiting for transfers between devices, refer_racks_in(): all_to_all(jnp.stack([m] * axis_size(comm_axis)), comm_axis, split_axis=0...  68.8 us
    all_gather x1, waiting for transfers between devices, per_device(): lax.all_gather(qkv_weight, 'frames', axis=1, tiled=True)[0]  61.4 us
    all_to_all x1, waiting for transfers between devices, per_device(): lax.all_to_all(grouped, BOOK, split_axis=0, concat_axis=2, tiled=True)  27.8 us
    all_to_all x1, starting transfers between devices, per_device(): lax.all_to_all(grouped, BOOK, split_axis=0, concat_axis=2, tiled=True)  12.8 us
    all_to_all x1, starting transfers between devices, refer_racks_in(): all_to_all(jnp.stack([m] * axis_size(comm_axis)), comm_axis, split_axis=0...  12.7 us
  transfers between devices with their start and end apart: 7, of which 7 were waited for; matrix products, arithmetic and copies ran while one was open for 5% of the time, Pallas kernels for 0%

profile of v1, /device:TPU:40, one launch (start us, length us, event | category | flops | bytes accessed | tf_op | source)
XLA Modules:
  0.0 408.6 jit_solution(712892694039130844)
XLA Ops:
  7.4 0.0 copy-start
  7.4 0.0 reduce-scatter.3.cloned.1.call-start
  7.4 1.9 copy-done
  9.3 4.3 %fusion.39 = f32[256,4096]{1,0:T(8,128)} fusion(bf16[384,4096]{1,0:T(8,128)(2,1)S(1)} %copy-done, bf16[256,384]{1,0:T(8,128)(2,1)} %param.11, bf16[256,384]{1,0:T(8,128)(2,1)} %param.10), kind=kOutput, calls=%fused_computation.43 | convolution fusion | flops 806092800 | bytes 7733248 | tf_op jit(solution)/shard_map/dot_general | solution.py:82
  13.5 0.0 copy-start.1
  13.5 0.0 reduce-scatter.3.cloned.1.call-update
  13.5 0.0 reduce-scatter.5.cloned.1.call-start
  13.6 63.1 %reduce-scatter.3.cloned.1.call-done = f32[256,512]{1,0:T(8,128)} async-done(((f32[256,4096]{1,0:T(8,128)}), f32[256,512]{1,0:T(8,128)}) %reduce-scatter.3.cloned.1.call-update) | async-done | bytes 524304 | tf_op jit(solution)/shard_map/reduce_scatter | solution.py:24
  76.6 0.0 reduce-scatter.5.cloned.1.call-update
  76.7 0.0 all-gather.4.cloned.1.call-start
  76.7 0.5 all-gather.4.cloned.1.call-update
  77.3 0.0 all-gather.6.cloned.1.call-start
  77.3 0.5 all-gather.6.cloned.1.call-update
  77.8 0.0 all-gather.8.cloned.1.call-start
  77.9 0.5 all-gather.8.cloned.1.call-update
  78.4 27.5 %reduce-scatter.5.cloned.1.call-done = f32[256,256]{1,0:T(8,128)} async-done(((f32[256,512]{1,0:T(8,128)}), f32[256,256]{1,0:T(8,128)}) %reduce-scatter.5.cloned.1.call-update) | async-done | bytes 262160 | tf_op jit(solution)/shard_map/reduce_scatter | solution.py:24
  105.9 0.0 copy-done.1
  105.9 1.0 add_convert_fusion
  106.9 0.1 copy.19
  107.0 0.0 copy-start.2
  107.0 0.0 copy-start.3
  107.0 1.5 stack.2
  108.5 12.7 %all-to-all-start = ((bf16[16,256,256]{1,2,0:T(8,128)(2,1)}), bf16[16,256,256]{1,2,0:T(8,128)(2,1)}, u32[]{:S(2)}, u32[]{:S(2)}) async-start(bf16[16,256,256]{1,2,0:T(8,128)(2,1)} %stack.2), calls=%async_computation.2 | async-start | bytes 4194304 | tf_op jit(solution)/shard_map/all_to_all | solution.py:16
  121.2 0.0 copy-done.2
  121.3 0.0 copy-done.3
  121.3 68.8 %all-to-all-done = bf16[16,256,256]{1,2,0:T(8,128)(2,1)} async-done(((bf16[16,256,256]{1,2,0:T(8,128)(2,1)}), bf16[16,256,256]{1,2,0:T(8,128)(2,1)}, u32[]{:S(2)}, u32[]{:S(2)}) %all-to-all-start) | async-done | bytes 2097184 | tf_op jit(solution)/shard_map/all_to_all | solution.py:16
  190.1 2.2 fusion.3
  192.3 2.9 fusion.5
  195.2 4.8 %all-gather.4.cloned.1.call-done = bf16[1,4096,1024]{2,1,0:T(8,128)(2,1)} async-done(((bf16[1,128,1024]{2,1,0:T(8,128)(2,1)}), bf16[1,4096,1024]{2,1,0:T(8,128)(2,1)}) %all-gather.4.cloned.1.call-update) | async-done | bytes 8388624 | tf_op jit(solution)/shard_map/all_gather | solution.py:91
  200.0 0.0 copy-start.4
  200.0 7.4 %fusion.1 = f32[256,1024]{1,0:T(8,128)} fusion(bf16[256,4096]{0,1:T(8,128)(2,1)} %bitcast.42, bf16[1,4096,1024]{2,1,0:T(8,128)(2,1)} %all-gather.4.cloned.1.call-done), kind=kOutput, calls=%fused_computation.1 | convolution fusion | flops 2147483648 | bytes 11534336 | tf_op jit(solution)/shard_map/dot_general | solution.py:89
  207.4 69.0 %all-gather.6.cloned.1.call-done = bf16[1,1024,1024]{2,1,0:T(8,128)(2,1)} async-done(((bf16[1,32,1024]{2,1,0:T(8,128)(2,1)}), bf16[1,1024,1024]{2,1,0:T(8,128)(2,1)}) %all-gather.6.cloned.1.call-update) | async-done | bytes 2097168 | tf_op jit(solution)/shard_map/all_gather | solution.py:58
  276.4 0.0 copy-done.4
  276.4 3.4 fusion.23
  279.9 61.4 %all-gather.8.cloned.1.call-done = bf16[1,1024,1536]{2,1,0:T(8,128)(2,1)} async-done(((bf16[1,32,1536]{2,1,0:T(8,128)(2,1)}), bf16[1,1024,1536]{2,1,0:T(8,128)(2,1)}) %all-gather.8.cloned.1.call-update) | async-done | bytes 3145744 | tf_op jit(solution)/shard_map/all_gather | solution.py:101
  341.2 4.0 fusion.8
  345.2 12.8 %all-to-all-start.1 = ((bf16[16,16,1,1536]{3,1,2,0:T(8,128)(2,1)}), bf16[16,16,1,1536]{3,1,2,0:T(8,128)(2,1)}, u32[]{:S(2)}, u32[]{:S(2)}) async-start(bf16[16,16,1,1536]{3,1,2,0:T(8,128)(2,1)} %bitcast.43), calls=%async_computation.3 | async-start | bytes 1572864 | tf_op jit(solution)/shard_map/all_to_all | solution.py:105
  358.0 27.8 %all-to-all-done.1 = bf16[16,16,1,1536]{3,1,2,0:T(8,128)(2,1)} async-done(((bf16[16,16,1,1536]{3,1,2,0:T(8,128)(2,1)}), bf16[16,16,1,1536]{3,1,2,0:T(8,128)(2,1)}, u32[]{:S(2)}, u32[]{:S(2)}) %all-to-all-start.1) | async-done | bytes 786464 | tf_op jit(solution)/shard_map/all_to_all | solution.py:105
  385.7 1.9 fusion.43
  387.7 2.1 reshape.62
  389.8 2.1 reshape.63
  391.8 1.1 reshape.61
  392.9 3.2 fusion.44
  396.1 1.9 fusion.22
  398.0 0.9 copy.28
  398.9 2.1 convert_element_type.77
  (5 shorter events, 0.0 us)
Async XLA Ops:
  7.4 1.9 copy-start
  7.4 69.3 %reduce-scatter.3.cloned.1.call-start = ((), (), s32[]{:S(2)}) async-start(), calls=%async_computation.4 | async-start | bytes 4718592 | tf_op jit(solution)/shard_map/reduce_scatter | solution.py:24
  13.5 92.4 %copy-start.1 = (bf16[256,256]{1,0:T(8,128)(2,1)S(1)}, bf16[256,256]{1,0:T(8,128)(2,1)}, u32[]{:S(2)}) copy-start(bf16[256,256]{1,0:T(8,128)(2,1)} %param.13) | copy-start | bytes 393220
  13.5 92.3 %reduce-scatter.5.cloned.1.call-start = ((), (), s32[]{:S(2)}) async-start(), calls=%async_computation.5 | async-start | bytes 786432 | tf_op jit(solution)/shard_map/reduce_scatter | solution.py:24
  76.7 123.4 %all-gather.4.cloned.1.call-start = ((), (), s32[]{:S(2)}) async-start(), calls=%async_computation.6 | async-start | bytes 8650752 | tf_op jit(solution)/shard_map/all_gather | solution.py:91
  77.3 199.2 %all-gather.6.cloned.1.call-start = ((), (), s32[]{:S(2)}) async-start(), calls=%async_computation.7 | async-start | bytes 2162688 | tf_op jit(solution)/shard_map/all_gather | solution.py:58
  77.8 263.4 %all-gather.8.cloned.1.call-start = ((), (), s32[]{:S(2)}) async-start(), calls=%async_computation.8 | async-start | bytes 3244032 | tf_op jit(solution)/shard_map/all_gather | solution.py:101
  107.0 14.3 %copy-start.2 = (bf16[4096]{0:T(1024)(128)(2,1)S(1)}, bf16[4096]{0:T(1024)(128)(2,1)}, u32[]{:S(2)}) copy-start(bf16[4096]{0:T(1024)(128)(2,1)} %param.14) | copy-start | bytes 24580
  107.0 14.3 %copy-start.3 = (bf16[1,1024]{1,0:T(2,128)(2,1)S(1)}, bf16[1,1024]{1,0:T(2,128)(2,1)}, u32[]{:S(2)}) copy-start(bf16[1,1024]{1,0:T(2,128)(2,1)} %param.18) | copy-start | bytes 6148
  108.5 81.6 %all-to-all-start = ((bf16[16,256,256]{1,2,0:T(8,128)(2,1)}), bf16[16,256,256]{1,2,0:T(8,128)(2,1)}, u32[]{:S(2)}, u32[]{:S(2)}) async-start(bf16[16,256,256]{1,2,0:T(8,128)(2,1)} %stack.2), calls=%async_computation.2 | async-start | bytes 4194304 | tf_op jit(solution)/shard_map/all_to_all | solution.py:16
  200.0 76.4 %copy-start.4 = (s32[256,1]{0,1:T(1,128)S(1)}, s32[256,1]{0,1:T(1,128)}, u32[]{:S(2)}) copy-start(s32[256,1]{0,1:T(1,128)} %param.17) | copy-start | bytes 3076
  345.2 40.5 %all-to-all-start.1 = ((bf16[16,16,1,1536]{3,1,2,0:T(8,128)(2,1)}), bf16[16,16,1,1536]{3,1,2,0:T(8,128)(2,1)}, u32[]{:S(2)}, u32[]{:S(2)}) async-start(bf16[16,16,1,1536]{3,1,2,0:T(8,128)(2,1)} %bitcast.43), calls=%async_computation.3 | async-start | bytes 1572864 | tf_op jit(solution)/shard_map/all_to_all | solution.py:105
Sparse Core Ops, SparseCore 0:
  13.7 62.9 reduce-scatter.2
  79.4 26.3 reduce-scatter.4
Sparse Core Ops, SparseCore 1:
  79.3 120.7 all-gather.3
  202.0 74.3 all-gather.5
  278.4 62.7 all-gather.7
